TPU v7x, 32 devices: a whole 2x2x4 slice. The times are simulated.
32 devices in a mesh: groups: 2 (over y), ctx: 4 (over z), head: 2 (over x), sub: 2 (over core).
Axes of the slice: x: 2, y: 2, z: 4, core: 2. Of those that a mesh axis runs over, the one named last changes fastest.
Arguments:
- queries: float32 [1024, 32, 128], P(('groups', 'ctx'), ('head', 'sub')), parts along dimension 0, may hold values from -110 to 110
- key_vectors: float32 [1024, 8, 128], P(('groups', 'ctx'), 'head'), parts along dimension 0, may hold values from -110 to 110
- value_vectors: float32 [1024, 8, 128], P(('groups', 'ctx'), 'head'), parts along dimension 0, may hold values from -20 to 20
- query_feature: float32 [32, 128, 128], P(('head', 'sub')), may hold values from -0.5 to 0.5
- key_feature: float32 [32, 128, 128], P(('head', 'sub')), may hold values from -0.5 to 0.5
Outputs:
- query_grad: float32 [1024, 32, 128], P(('groups', 'ctx'), ('head', 'sub')), parts along dimension 0
- key_grad: float32 [1024, 8, 128], P(('groups', 'ctx'), 'head'), parts along dimension 0
- value_grad: float32 [1024, 8, 128], P(('groups', 'ctx'), 'head'), parts along dimension 0
There are 2 independent parts, one for each index of `groups`. A program takes and returns all parts, laid end to end along the dimension named above; an argument that names none is the same for every part. Nothing has to cross between parts.
All inputs are finite; a program needn't handle non-finite values.
Results may differ from a plain program's by a relative error of at most 0.0003.
Values sent between devices are 32-bit elements; how exact they have to be, the bound alone decides.
No kernel may reach another device: no remote copies, remote signals or barrier semaphores. Data moves between devices by JAX's collectives and lax.ppermute only.
A program may use at most 64 MiB of HBM per device.

v0:
```python
import math

import jax
import jax.numpy as jnp
from jax import lax
from jax.sharding import PartitionSpec as P

BLK = 128


highest = lax.Precision.HIGHEST
neg_large = -1e30


def from_behind(value, axis, steps):
    count = lax.axis_size(axis)
    leading, last = (max(0, -steps), min(count, count - steps))
    return lax.ppermute(value, axis, [(source, source + steps) for source in range(leading, last)])


def from_partner(value, axis, stride):
    return lax.ppermute(value, axis, [(i, i ^ 1 << stride) for i in range(lax.axis_size(axis))])


def carried_in(value, axis, combine, identity, reverse):
    devices, here = (lax.axis_size(axis), lax.axis_index(axis))
    everything = jax.tree.map(lambda part: lax.all_gather(part, axis), value)
    start = jax.tree.map(
        lambda part, zero: jnp.broadcast_to(jnp.asarray(zero, part.dtype), part.shape),
        value,
        identity,
    )

    def hop(k, before):
        at = devices - 1 - k if reverse else k
        reached = at > here if reverse else at < here
        new = combine(before, jax.tree.map(lambda part: part[at], everything))
        return jax.tree.map(lambda a, b: jnp.where(reached, a, b), new, before)

    return lax.fori_loop(0, devices, hop, start)


def features(rows, weight):
    mapped = jnp.einsum("lnd,lde->lne", rows, weight, precision=highest)
    joined = jnp.concatenate(
        [jax.nn.softmax(mapped, axis=-1), jax.nn.softmax(-mapped, axis=-1)], axis=-1
    )
    return (joined, mapped)


def features_back(mapped, weight, grad_feat):
    width = mapped.shape[-1]
    upper = jax.nn.softmax(mapped, axis=-1)
    lower = jax.nn.softmax(-mapped, axis=-1)
    grad_upper = grad_feat[..., :width]
    grad_lower = grad_feat[..., width:]
    grad_mapped = upper * (grad_upper - jnp.sum(upper * grad_upper, axis=-1, keepdims=True))
    grad_mapped = grad_mapped - lower * (
        grad_lower - jnp.sum(lower * grad_lower, axis=-1, keepdims=True)
    )
    return jnp.einsum("lne,lde->lnd", grad_mapped, weight, precision=highest)


def fold_keys(carry, query_heads, rows_key, rows_value, positions, query_pos, pick, score_scale):
    count = rows_key.shape[0]
    step = 512 if count % 512 == 0 else count

    def one_block(state, block_in):
        keys_raw, values_raw, pos_block = block_in
        keys_heads = jnp.einsum("ngd,lg->lnd", keys_raw, pick, precision=highest)
        values_heads = jnp.einsum("ngd,lg->lnd", values_raw, pick, precision=highest)
        logit_scores = (
            jnp.einsum("ltd,lnd->ltn", query_heads, keys_heads, precision=highest) * score_scale
        )
        allowed = pos_block[None, None, :] <= query_pos[None, :, None]
        best, mass, weighted = state
        top = jnp.maximum(best, jnp.max(jnp.where(allowed, logit_scores, neg_large), axis=-1))
        weights = jnp.exp(jnp.where(allowed, logit_scores - top[..., None], neg_large))
        factor = jnp.exp(best - top)
        mass = mass * factor + jnp.sum(weights, axis=-1)
        weighted = weighted * factor[..., None] + jnp.einsum(
            "ltn,lnd->ltd", weights, values_heads, precision=highest
        )
        return ((top, mass, weighted), None)

    blocks = count // step
    stacked = (
        rows_key.reshape((blocks, step) + rows_key.shape[1:]),
        rows_value.reshape((blocks, step) + rows_value.shape[1:]),
        positions.reshape((blocks, step)),
    )
    carry, _ = lax.scan(one_block, carry, stacked)
    return carry


def add_pair(earlier, later):
    return (earlier[0] + later[0], earlier[1] + later[1])


def empty_carry(heads, rows, width):
    return (
        jnp.full((heads, rows), neg_large, jnp.float32),
        jnp.zeros((heads, rows), jnp.float32),
        jnp.zeros((heads, rows, width), jnp.float32),
    )


def local(queries, key_vectors, value_vectors, query_feature, key_feature):
    tokens, heads_dev, width = queries.shape
    groups_dev = key_vectors.shape[1]
    feat_width = 2 * width
    blocks_dev = tokens // BLK
    score_scale = 1.0 / math.sqrt(width)
    ctx_index = lax.axis_index("ctx")
    sub_index = lax.axis_index("sub")
    sub_count = lax.axis_size("sub")
    group_size = heads_dev * sub_count // groups_dev
    own_heads = sub_index * heads_dev + jnp.arange(heads_dev)
    selector = (own_heads[:, None] // group_size == jnp.arange(groups_dev)[None, :]).astype(
        jnp.float32
    )
    query_heads = jnp.transpose(queries, (1, 0, 2))
    query_pos = ctx_index * tokens + jnp.arange(tokens)
    previous = from_behind((key_vectors, value_vectors), "ctx", 1)
    key_ext = jnp.concatenate([previous[0], key_vectors], axis=0)
    value_ext = jnp.concatenate([previous[1], value_vectors], axis=0)
    key_heads = jnp.einsum("tgd,lg->ltd", key_ext, selector, precision=highest)
    value_heads = jnp.einsum("tgd,lg->ltd", value_ext, selector, precision=highest)
    joined = lax.all_gather(queries, "sub", axis=1, tiled=True)
    joined_heads = jnp.transpose(joined, (1, 0, 2))
    pair_heads = joined_heads.shape[0]
    pair_pick = (
        jnp.arange(pair_heads)[:, None] // group_size == jnp.arange(groups_dev)[None, :]
    ).astype(jnp.float32)
    half = tokens // sub_count
    key_half = lax.dynamic_slice_in_dim(key_vectors, sub_index * half, half, 0)
    value_half = lax.dynamic_slice_in_dim(value_vectors, sub_index * half, half, 0)
    initial = empty_carry(pair_heads, tokens, width)
    piece = (
        lax.all_gather(key_half, "ctx", axis=0, tiled=True),
        lax.all_gather(value_half, "ctx", axis=0, tiled=True),
    )
    rows = piece[0].shape[0]
    gathered_index = jnp.arange(rows)
    positions = gathered_index // half * tokens + sub_index * half + gathered_index % half
    best_all, mass_all, weighted_all = fold_keys(
        initial, joined_heads, piece[0], piece[1], positions, query_pos, pair_pick, score_scale
    )
    other_start = (1 - sub_index) * heads_dev
    own_start = sub_index * heads_dev
    sent = (
        lax.dynamic_slice_in_dim(best_all, other_start, heads_dev, 0),
        lax.dynamic_slice_in_dim(mass_all, other_start, heads_dev, 0),
        lax.dynamic_slice_in_dim(weighted_all, other_start, heads_dev, 0),
    )
    got = from_partner((sent[0], sent[1], sent[2]), "sub", 0)
    own_best = lax.dynamic_slice_in_dim(best_all, own_start, heads_dev, 0)
    own_mass = lax.dynamic_slice_in_dim(mass_all, own_start, heads_dev, 0)
    own_weighted = lax.dynamic_slice_in_dim(weighted_all, own_start, heads_dev, 0)
    best = jnp.maximum(own_best, got[0])
    own_factor = jnp.exp(own_best - best)
    got_factor = jnp.exp(got[0] - best)
    mass = own_mass * own_factor + got[1] * got_factor
    weighted = own_weighted * own_factor[..., None] + got[2] * got_factor[..., None]
    target = weighted / mass[..., None]
    query_feature_rows, query_mapped = features(query_heads, query_feature)
    key_feat, key_mapped = features(key_heads, key_feature)
    has_prev = (ctx_index > 0).astype(jnp.float32)
    block_live = jnp.where(jnp.arange(blocks_dev + 1) == 0, has_prev, 1.0)
    feat_blocks = key_feat.reshape(heads_dev, blocks_dev + 1, BLK, feat_width)
    value_blocks = value_heads.reshape(heads_dev, blocks_dev + 1, BLK, width)
    block_states = jnp.einsum("lbnf,lbnd->lbfd", feat_blocks, value_blocks, precision=highest)
    block_states = block_states * block_live[None, :, None, None]
    block_norms = jnp.sum(feat_blocks, axis=2) * block_live[None, :, None]
    send_state = jnp.sum(block_states[:, :blocks_dev], axis=1)
    send_norm = jnp.sum(block_norms[:, :blocks_dev], axis=1)
    carried_state, carried_norm = carried_in(
        (send_state, send_norm),
        "ctx",
        add_pair,
        (jnp.zeros_like(send_state), jnp.zeros_like(send_norm)),
        False,
    )
    lead_states = jnp.cumsum(block_states[:, : blocks_dev - 1], axis=1)
    lead_norms = jnp.cumsum(block_norms[:, : blocks_dev - 1], axis=1)
    query_state = carried_state[:, None] + jnp.concatenate(
        [jnp.zeros((heads_dev, 1, feat_width, width), jnp.float32), lead_states], axis=1
    )
    query_norm = carried_norm[:, None] + jnp.concatenate(
        [jnp.zeros((heads_dev, 1, feat_width), jnp.float32), lead_norms], axis=1
    )
    key_blocks = key_heads.reshape(heads_dev, blocks_dev + 1, BLK, width)
    local_window_keys = jnp.concatenate([key_blocks[:, :-1], key_blocks[:, 1:]], axis=2)
    local_window_values = jnp.concatenate([value_blocks[:, :-1], value_blocks[:, 1:]], axis=2)
    query_block_list = query_heads.reshape(heads_dev, blocks_dev, BLK, width)
    feat_q_blocks = query_feature_rows.reshape(heads_dev, blocks_dev, BLK, feat_width)
    logit_scores = (
        jnp.einsum("lbqd,lbkd->lbqk", query_block_list, local_window_keys, precision=highest)
        * score_scale
    )
    row = jnp.arange(BLK)
    column = jnp.arange(2 * BLK)
    prev_ok = (jnp.arange(blocks_dev) > 0) | (ctx_index > 0)
    allowed = jnp.where(
        column[None, None, :] < BLK,
        prev_ok[:, None, None],
        column[None, None, :] - BLK <= row[None, :, None],
    )
    top = jnp.max(jnp.where(allowed, logit_scores, neg_large), axis=-1)
    softmax_probs = jnp.exp(jnp.where(allowed, logit_scores - top[..., None], neg_large))
    numerator = jnp.einsum("lbqk,lbkd->lbqd", softmax_probs, local_window_values, precision=highest)
    numerator = numerator + jnp.einsum(
        "lbqf,lbfd->lbqd", feat_q_blocks, query_state, precision=highest
    )
    denom = jnp.sum(softmax_probs, axis=-1) + jnp.einsum(
        "lbqf,lbf->lbq", feat_q_blocks, query_norm, precision=highest
    )
    output = numerator / denom[..., None]
    residual_grad = output - target.reshape(heads_dev, blocks_dev, BLK, width)
    grad_numer = residual_grad / denom[..., None]
    grad_denom = -jnp.sum(residual_grad * output, axis=-1) / denom
    grad_soft = (
        jnp.einsum("lbqd,lbkd->lbqk", grad_numer, local_window_values, precision=highest)
        + grad_denom[..., None]
    )
    grad_scores = softmax_probs * grad_soft * score_scale
    grad_query_win = jnp.einsum(
        "lbqk,lbkd->lbqd", grad_scores, local_window_keys, precision=highest
    )
    grad_key_win = jnp.einsum("lbqk,lbqd->lbkd", grad_scores, query_block_list, precision=highest)
    grad_value_win = jnp.einsum("lbqk,lbqd->lbkd", softmax_probs, grad_numer, precision=highest)
    zero_block = jnp.zeros((heads_dev, 1, BLK, width), jnp.float32)
    grad_key_ext = jnp.concatenate(
        [grad_key_win[:, :, :BLK], zero_block], axis=1
    ) + jnp.concatenate([zero_block, grad_key_win[:, :, BLK:]], axis=1)
    grad_value_ext = jnp.concatenate(
        [grad_value_win[:, :, :BLK], zero_block], axis=1
    ) + jnp.concatenate([zero_block, grad_value_win[:, :, BLK:]], axis=1)
    grad_qfeat = jnp.einsum("lbqd,lbfd->lbqf", grad_numer, query_state, precision=highest)
    grad_qfeat = grad_qfeat + grad_denom[..., None] * query_norm[:, :, None, :]
    query_terms = jnp.einsum("lbqf,lbqd->lbfd", feat_q_blocks, grad_numer, precision=highest)
    query_sums = jnp.einsum("lbqf,lbq->lbf", feat_q_blocks, grad_denom, precision=highest)
    back_state = jnp.sum(query_terms, axis=1)
    back_norm = jnp.sum(query_sums, axis=1)
    later_state, later_norm = carried_in(
        (back_state, back_norm),
        "ctx",
        add_pair,
        (jnp.zeros_like(back_state), jnp.zeros_like(back_norm)),
        True,
    )
    back_key = jnp.einsum("lnd,lg->ngd", grad_key_ext[:, 0], selector, precision=highest)
    back_value = jnp.einsum("lnd,lg->ngd", grad_value_ext[:, 0], selector, precision=highest)
    arrived_back = from_behind(
        (back_key, back_value, query_terms[:, 0], query_sums[:, 0]), "ctx", -1
    )
    suffix_terms = jnp.flip(jnp.cumsum(jnp.flip(query_terms, axis=1), axis=1), axis=1)
    suffix_sums = jnp.flip(jnp.cumsum(jnp.flip(query_sums, axis=1), axis=1), axis=1)
    skip_terms = jnp.concatenate(
        [suffix_terms[:, 2:], jnp.zeros((heads_dev, 2, feat_width, width), jnp.float32)], axis=1
    )[:, :blocks_dev]
    skip_sums = jnp.concatenate(
        [suffix_sums[:, 2:], jnp.zeros((heads_dev, 2, feat_width), jnp.float32)], axis=1
    )[:, :blocks_dev]
    last_flag = (jnp.arange(blocks_dev) == blocks_dev - 1).astype(jnp.float32)
    key_state = (
        later_state[:, None]
        + skip_terms
        - last_flag[None, :, None, None] * arrived_back[2][:, None]
    )
    key_norm = later_norm[:, None] + skip_sums - last_flag[None, :, None] * arrived_back[3][:, None]
    own_feat = key_feat[:, BLK:].reshape(heads_dev, blocks_dev, BLK, feat_width)
    own_values = value_blocks[:, 1:]
    grad_kfeat = (
        jnp.einsum("lbfd,lbnd->lbnf", key_state, own_values, precision=highest)
        + key_norm[:, :, None, :]
    )
    grad_value_lin = jnp.einsum("lbnf,lbfd->lbnd", own_feat, key_state, precision=highest)
    grad_query_rows = features_back(
        query_mapped, query_feature, grad_qfeat.reshape(heads_dev, tokens, feat_width)
    )
    grad_key_rows = features_back(
        key_mapped[:, BLK:], key_feature, grad_kfeat.reshape(heads_dev, tokens, feat_width)
    )
    query_grad = jnp.transpose(
        grad_query_win.reshape(heads_dev, tokens, width) + grad_query_rows, (1, 0, 2)
    )
    key_head_grad = grad_key_ext[:, 1:].reshape(heads_dev, tokens, width) + grad_key_rows
    value_head_grad = (grad_value_ext[:, 1:] + grad_value_lin).reshape(heads_dev, tokens, width)
    key_local = jnp.einsum("ltd,lg->tgd", key_head_grad, selector, precision=highest)
    value_local = jnp.einsum("ltd,lg->tgd", value_head_grad, selector, precision=highest)
    key_local = key_local + arrived_back[0]
    value_local = value_local + arrived_back[1]
    key_grad, value_grad = lax.psum((key_local, value_local), "sub")
    return (query_grad, key_grad, value_grad)


def solution(mesh):
    placed = (
        P(("groups", "ctx"), ("head", "sub"), None),
        P(("groups", "ctx"), "head", None),
        P(("groups", "ctx"), "head", None),
        P(("head", "sub"), None, None),
        P(("head", "sub"), None, None),
    )
    return jax.shard_map(
        local,
        mesh=mesh,
        in_specs=placed,
        out_specs=(
            P(("groups", "ctx"), ("head", "sub"), None),
            P(("groups", "ctx"), "head", None),
            P(("groups", "ctx"), "head", None),
        ),
        check_vma=False,
    )
```

profile of v0, /device:TPU:0, one launch (start us, length us, event | category | flops | bytes accessed | tf_op | source)
XLA Modules:
  0.0 309.4 jit_solution(12048689764705509977)
XLA Ops:
  7.2 5.1 %collective-permute-start = (f32[128,4,128]{2,1,0:T(4,128)}, f32[128,4,128]{2,1,0:T(4,128)S(1)}, u32[]{:S(2)}, u32[]{:S(2)}) collective-permute-start(f32[128,4,128]{2,1,0:T(4,128)} %param.10), channel_id=1, source_target_pairs={{0,4},{4,8},{8,12},{1,5},{5,9},{9,13},{2,6},{6,10},{10,14},{3,7},{... | collective-permute-start | bytes 786440 | tf_op jit(solution)/shard_map/ppermute | solution.py:18
  12.3 3.5 %collective-permute-start.1 = (f32[128,4,128]{2,1,0:T(4,128)}, f32[128,4,128]{2,1,0:T(4,128)S(1)}, u32[]{:S(2)}, u32[]{:S(2)}) collective-permute-start(f32[128,4,128]{2,1,0:T(4,128)} %param.11), channel_id=1, source_target_pairs={{0,4},{4,8},{8,12},{1,5},{5,9},{9,13},{2,6},{6,10},{10,14},{3,7},{... | collective-permute-start | bytes 786440 | tf_op jit(solution)/shard_map/ppermute | solution.py:18
  32.0 18.2 %all_gather.37 = f32[256,4,128]{2,1,0:T(4,128)S(1)} all-gather(f32[64,4,128]{2,1,0:T(4,128)S(1)} %constant_dynamic-slice_fusion.4), channel_id=1, replica_groups=mesh['groups'=2,'ctx'=4,'head'=2,'sub'=2] {'ctx'}, dimensions={0}, use_global_device_ids=true | all-gather | bytes 655360 | tf_op jit(solution)/shard_map/all_gather | solution.py:140
  50.1 23.5 %all_gather.39 = f32[256,4,128]{2,1,0:T(4,128)S(1)} all-gather(f32[64,4,128]{2,1,0:T(4,128)S(1)} %constant_dynamic-slice_fusion.3), channel_id=1, replica_groups=mesh['groups'=2,'ctx'=4,'head'=2,'sub'=2] {'ctx'}, dimensions={0}, use_global_device_ids=true | all-gather | bytes 655360 | tf_op jit(solution)/shard_map/all_gather | solution.py:141
  76.8 2.4 fusion.128
  79.2 2.4 fusion.126
  81.6 3.3 %reshape.364 = f32[8,2,128,256]{2,1,3,0:T(2,128)} reshape(f32[8,256,256]{1,2,0:T(8,128)} %get-tuple-element.394) | data formatting | bytes 4194304 | tf_op jit(solution)/shard_map/reshape | solution.py:170
  84.9 5.0 %reduce_sum.133 = f32[8,2,256]{1,2,0:T(8,128)} reduce(f32[8,2,128,256]{2,1,3,0:T(2,128)} %reshape.364, f32[]{:T(128)} %constant.174.clone.1), dimensions={2}, to_apply=%region_9.10 | reduce | flops 520192 | bytes 2113540 | tf_op jit(solution)/shard_map/reduce_sum | solution.py:174
  91.5 14.2 %all-gather.1 = f32[32,1,256]{2,1,0:T(1,128)S(1)} all-gather(f32[8,1,256]{2,1,0:T(1,128)S(1)} %copy.164), channel_id=3, replica_groups=mesh['groups'=2,'ctx'=4,'head'=2,'sub'=2] {'ctx'}, dimensions={0}, use_global_device_ids=true | all-gather | bytes 40960 | tf_op jit(solution)/shard_map/all_gather | solution.py:27
  114.0 2.6 select_reduce_fusion
  116.8 2.2 fusion.55
  119.1 4.5 %fusion.9 = (f32[16,128]{1,0:T(8,128)S(1)}, f32[16,256,128]{2,1,0:T(8,128)S(1)}) fusion(pred[128,256]{0,1:T(8,128)(4,1)S(1)} %broadcast_compare_fusion, f32[128,16,128]{2,0,1:T(8,128)} %all-gather.8.cloned.1.call-done, f32[16,256,128]{2,0,1:T(8,128)} %fusion.128), kind=kOutput, calls=%fused_computation.18 | convolution fusion | flops 806877184 | bytes 5283840 | tf_op jit(solution)/shard_map/while/body/eval_jaxpr/ltd,lnd->ltn/dot_general | solution.py:73
  125.2 4.5 %fusion.25 = f32[16,128,128]{1,2,0:T(8,128)S(1)} fusion(f32[16,256,128]{2,0,1:T(8,128)S(1)} %copy-done.21, f32[16,256,128]{2,1,0:T(8,128)S(1)} %get-tuple-element.417, f32[16,128]{1,0:T(8,128)S(1)} %broadcast_maximum_fusion, pred[128,256]{0,1:T(8,128)(4,1)S(1)} %broadcast_compare_fusion, f32[16,128]{1,0:T(8,128)S(1)} %get-tuple-element.404), kind=kOutput, calls=%fused_computation.39 | convolution fusion | flops 807141376 | bytes 5292032 | tf_op jit(solution)/shard_map/while/body/eval_jaxpr/ltn,lnd->ltd/dot_general | solution.py:81
  130.9 6.7 %while.40 = (s32[]{:T(128)}, f32[8,256,128]{2,1,0:T(8,128)S(1)}, f32[8,256]{1,0:T(8,128)S(1)}, s32[]{:T(128)}, f32[4,8,256,128]{3,2,1,0:T(8,128)}, /*index=5*/f32[4,8,256]{2,1,0:T(8,128)S(1)}, s32[]{:T(128)}, s32[]{:T(128)}) while((s32[]{:T(128)}, f32[8,256,128]{2,1,0:T(8,128)S(1)}, f32[8,256]{1,0:T(8,128)S(1)}, s32[]{:T(128)}, ...), condition=%wide.region_11.12_spmd.clone, body=%wide.region_10.11_spmd.clone.sunk | while | flops 792580 | bytes 3170419 | solution.py:40
  138.4 3.4 %multiply_reduce_fusion.4 = (f32[8,128]{1,0:T(8,128)S(1)}, f32[8,128,128]{1,2,0:T(8,128)S(1)}) fusion(f32[8,128]{1,0:T(8,128)S(1)} %get-tuple-element.389, f32[8,128,128]{1,2,0:T(8,128)} %collective-permute-done.3, f32[8,128]{1,0:T(8,128)S(1)} %get-tuple-element.391, f32[8,128]{1,0:T(8,128)S(1)} %get-tuple-element.390, f32[16,128,128]{1,2,0:T(8,128)} %copy-done.31, ...), kind=kOutput, calls=%fused_computation.119 | convolution fusion | flops 404225024 | bytes 4214788 | tf_op jit(solution)/shard_map/lbqf,lbfd->lbqd/dot_general | solution.py:212
  144.8 2.1 fusion.157
  163.4 96.6 %all-gather.3 = f32[32,256]{1,0:T(8,128)S(1)} all-gather(f32[8,256]{1,0:T(8,128)S(1)} %bitcast.154), channel_id=5, replica_groups=mesh['groups'=2,'ctx'=4,'head'=2,'sub'=2] {'ctx'}, dimensions={0}, use_global_device_ids=true | all-gather | bytes 40960 | tf_op jit(solution)/shard_map/all_gather | solution.py:27
  262.1 6.6 %while.41 = (s32[]{:T(128)}, f32[8,256,128]{2,1,0:T(8,128)S(1)}, f32[8,256]{1,0:T(8,128)S(1)}, s32[]{:T(128)}, f32[4,8,256,128]{3,2,1,0:T(8,128)}, /*index=5*/f3...) while((s32[]{:T(128)}, f32[8,256,128]{2,1,0:T(8,128)S(1)}, ...), condition=%wide.region_21.22_spmd.clone, body=%wide.region_20.21_spmd.clone.sunk | while | flops 792584 | bytes 3170481 | solution.py:40
  268.8 2.4 convolution_add_fusion
  273.3 3.2 %fusion.41 = f32[8,128,128]{2,1,0:T(8,128)S(1)} fusion(f32[8,256,128]{1,2,0:T(8,128)S(1)} %copy-done.13, f32[8,256,128]{1,2,0:T(8,128)S(1)} %copy-done.11, f32[8,1,128,128]{3,2,0,1:T(8,128)S(1)} %copy-done.28, f32[8,1,128,128]{3,2,0,1:T(8,128)S(1)} %copy-done.30, f32[8,256,128]{2,1,0:T(8,128)S(1)} %get-tuple-element.300, ...), kind=kOutput, calls=%fused_computation.55 | convolution fusion | flops 403439616 | bytes 5767168 | tf_op jit(solution)/shard_map/lbnf,lbfd->lbnd/dot_general | solution.py:278
  276.5 2.4 fusion.43
  278.9 2.4 fusion.42
  281.4 3.1 %fusion.56 = f32[8,128,128]{2,1,0:T(8,128)S(1)} fusion(f32[8,128,256]{1,2,0:T(8,128)S(1)} %copy-done.8, f32[8,1,128,128]{3,2,0,1:T(8,128)} %copy.215, f32[8,1,128,128]{3,2,0,1:T(8,128)S(1)} %copy-done.24), kind=kOutput, calls=%fused_computation.84 | convolution fusion | flops 402915328 | bytes 2621440 | tf_op jit(solution)/shard_map/lbqk,lbkd->lbqd/dot_general | solution.py:227
  286.7 12.4 %all-reduce.7.cloned.1.call-done = (f32[128,4,128]{2,1,0:T(4,128)}, f32[128,4,128]{2,1,0:T(4,128)}) async-done(((f32[128,4,128]{2,1,0:T(4,128)}, f32[128,4,128]{2,1,0:T(4,128)}), (f32[128,4,128]{2,1,0:T(4,128)}, f32[128,4,128]{2,1,0:T(4,128)})) %all-reduce.7.cloned.1.call-update) | async-done | bytes 524304 | tf_op jit(solution)/shard_map/psum | solution.py:294
  (199 shorter events, 74.2 us)
Async XLA Ops:
  7.2 13.9 %copy-start = (f32[8,128,128]{2,1,0:T(8,128)S(1)}, f32[8,128,128]{2,1,0:T(8,128)}, u32[]{:S(2)}) copy-start(f32[8,128,128]{2,1,0:T(8,128)} %param.13) | copy-start | bytes 1572868
  7.2 111.9 %all-gather.8.cloned.1.call-start = ((), (), s32[]{:S(2)}) async-start(), calls=%async_computation | async-start | bytes 1572864 | tf_op jit(solution)/shard_map/all_gather | solution.py:129
  7.2 12.1 %collective-permute-start = (f32[128,4,128]{2,1,0:T(4,128)}, f32[128,4,128]{2,1,0:T(4,128)S(1)}, u32[]{:S(2)}, u32[]{:S(2)}) collective-permute-start(f32[128,4,128]{2,1,0:T(4,128)} %param.10), channel_id=1, source_target_pairs={{0,4},{4,8},{8,12},{1,5},{5,9},{9,13},{2,6},{6,10},{10,14},{3,7},{... | collective-permute-start | bytes 786440 | tf_op jit(solution)/shard_map/ppermute | solution.py:18
  12.3 14.5 %collective-permute-start.1 = (f32[128,4,128]{2,1,0:T(4,128)}, f32[128,4,128]{2,1,0:T(4,128)S(1)}, u32[]{:S(2)}, u32[]{:S(2)}) collective-permute-start(f32[128,4,128]{2,1,0:T(4,128)} %param.11), channel_id=1, source_target_pairs={{0,4},{4,8},{8,12},{1,5},{5,9},{9,13},{2,6},{6,10},{10,14},{3,7},{... | collective-permute-start | bytes 786440 | tf_op jit(solution)/shard_map/ppermute | solution.py:18
  17.8 113.1 %all-gather.10.cloned.1.call-start = ((), (), s32[]{:S(2)}) async-start(), calls=%async_computation.1 | async-start | bytes 5242880 | tf_op jit(solution)/shard_map/all_gather | solution.py:27
  29.7 44.1 %copy-start.16 = (f32[128,8,128]{2,1,0:T(8,128)S(1)}, f32[128,8,128]{2,1,0:T(8,128)}, u32[]{:S(2)}) copy-start(f32[128,8,128]{2,1,0:T(8,128)} %param.9) | copy-start | bytes 1572868
  30.9 231.3 %all-gather.12.cloned.1.call-start = ((), (), s32[]{:S(2)}) async-start(), calls=%async_computation.2 | async-start | bytes 5242880 | tf_op jit(solution)/shard_map/all_gather | solution.py:27
  30.9 42.9 %copy-start.32 = (f32[8,128,128]{2,1,0:T(8,128)S(1)}, f32[8,128,128]{2,1,0:T(8,128)}, u32[]{:S(2)}) copy-start(f32[8,128,128]{2,1,0:T(8,128)} %param.12) | copy-start | bytes 1572868
  116.6 7.0 %copy-start.1 = (f32[8,128,256]{1,2,0:T(8,128)}, f32[8,128,256]{1,2,0:T(8,128)S(1)}, u32[]{:S(2)}) copy-start(f32[8,128,256]{1,2,0:T(8,128)S(1)} %get-tuple-element.407) | copy-start | bytes 3145732
  124.1 6.7 %collective-permute-start.4 = (f32[8,128]{1,0:T(8,128)S(1)}, f32[8,128]{1,0:T(8,128)S(1)}, u32[]{:S(2)}, u32[]{:S(2)}) collective-permute-start(f32[8,128]{1,0:T(8,128)S(1)} %constant_dynamic-slice_fusion), channel_id=1, source_target_pairs={{0,1},{1,0},{2,3},{3,2},{4,5},{5,4},{6,7},{7,6},{8,9},{9,8},{10,11... | collective-permute-start | bytes 12296 | tf_op jit(solution)/shard_map/ppermute | solution.py:22
  124.2 6.7 %collective-permute-start.2 = (f32[8,128]{1,0:T(8,128)S(1)}, f32[8,128]{1,0:T(8,128)S(1)}, u32[]{:S(2)}, u32[]{:S(2)}) collective-permute-start(f32[8,128]{1,0:T(8,128)S(1)} %constant_dynamic-slice_fusion.2), channel_id=1, source_target_pairs={{0,1},{1,0},{2,3},{3,2},{4,5},{5,4},{6,7},{7,6},{8,9},{9,8},{10,11... | collective-permute-start | bytes 12296 | tf_op jit(solution)/shard_map/ppermute | solution.py:22
  130.8 7.6 %collective-permute-start.3 = (f32[8,128,128]{1,2,0:T(8,128)S(1)}, f32[8,128,128]{1,2,0:T(8,128)}, u32[]{:S(2)}, u32[]{:S(2)}) collective-permute-start(f32[8,128,128]{1,2,0:T(8,128)S(1)} %constant_dynamic-slice_fusion.1), channel_id=1, source_target_pairs={{0,1},{1,0},{2,3},{3,2},{4,5},{5,4},{6,7},{7,6},{8,9},{9,8},{10,11... | collective-permute-start | bytes 1572872 | tf_op jit(solution)/shard_map/ppermute | solution.py:22
  130.9 6.8 %copy-start.3 = (f32[8,128,128]{1,2,0:T(8,128)S(1)}, f32[8,128,128]{1,2,0:T(8,128)}, u32[]{:S(2)}) copy-start(f32[8,128,128]{1,2,0:T(8,128)} %get-tuple-element.425) | copy-start | bytes 1572868
  144.7 154.4 %all-reduce.7.cloned.1.call-start = ((), (), s32[]{:S(2)}) async-start(), calls=%async_computation.3 | async-start | bytes 1048576 | tf_op jit(solution)/shard_map/psum | solution.py:294
  144.7 5.5 %copy-start.4 = (f32[8,128,128]{1,2,0:T(8,128)S(1)}, f32[8,128,128]{1,2,0:T(8,128)}, u32[]{:S(2)}) copy-start(f32[8,128,128]{1,2,0:T(8,128)} %get-tuple-element.425) | copy-start | bytes 1572868
  144.8 6.5 %copy-start.2 = (f32[8,128,256]{1,2,0:T(8,128)S(1)}, f32[8,128,256]{1,2,0:T(8,128)}, u32[]{:S(2)}) copy-start(f32[8,128,256]{1,2,0:T(8,128)} %copy-done.1) | copy-start | bytes 3145732
  144.8 6.5 %copy-start.15 = (f32[8,128,128]{1,2,0:T(8,128)S(1)}, f32[8,128,128]{1,2,0:T(8,128)}, u32[]{:S(2)}) copy-start(f32[8,128,128]{1,2,0:T(8,128)} %copy-done.14) | copy-start | bytes 1572868
  148.9 119.9 %collective-permute-start.5 = (f32[8,256,128]{2,1,0:T(8,128)}, f32[8,256,128]{2,1,0:T(8,128)}, u32[]{:S(2)}, u32[]{:S(2)}) collective-permute-start(f32[8,256,128]{2,1,0:T(8,128)} %fusion.92), channel_id=1, source_target_pairs={{4,0},{8,4},{12,8},{5,1},{9,5},{13,9},{6,2},{10,6},{14,10},{7,3},{... | collective-permute-start | bytes 3145736 | tf_op jit(solution)/shard_map/ppermute | solution.py:18
  153.4 6.0 %copy-start.17 = (f32[128,8,128]{2,1,0:T(8,128)S(1)}, f32[128,8,128]{2,1,0:T(8,128)}, u32[]{:S(2)}) copy-start(f32[128,8,128]{2,1,0:T(8,128)} %param.9) | copy-start | bytes 1572868
  154.8 121.7 %collective-permute-start.8 = (f32[128,4,128]{2,1,0:T(4,128)}, f32[128,4,128]{2,1,0:T(4,128)}, u32[]{:S(2)}, u32[]{:S(2)}) collective-permute-start(f32[128,4,128]{2,1,0:T(4,128)} %convolution_bitcast_fusion.3), channel_id=1, source_target_pairs={{4,0},{8,4},{12,8},{5,1},{9,5},{13,9},{6,2},{10,6},{14,10},{7,3},{... | collective-permute-start | bytes 786440 | tf_op jit(solution)/shard_map/ppermute | solution.py:18
  156.1 112.7 %collective-permute-start.6 = (f32[8,256]{1,0:T(8,128)S(1)}, f32[8,256]{1,0:T(8,128)S(1)}, u32[]{:S(2)}, u32[]{:S(2)}) collective-permute-start(f32[8,256]{1,0:T(8,128)S(1)} %bitcast.153), channel_id=1, source_target_pairs={{4,0},{8,4},{12,8},{5,1},{9,5},{13,9},{6,2},{10,6},{14,10},{7,3},{... | collective-permute-start | bytes 24584 | tf_op jit(solution)/shard_map/ppermute | solution.py:18
  162.0 116.9 %collective-permute-start.7 = (f32[128,4,128]{2,1,0:T(4,128)}, f32[128,4,128]{2,1,0:T(4,128)}, u32[]{:S(2)}, u32[]{:S(2)}) collective-permute-start(f32[128,4,128]{2,1,0:T(4,128)} %convolution_bitcast_fusion.5), channel_id=1, source_target_pairs={{4,0},{8,4},{12,8},{5,1},{9,5},{13,9},{6,2},{10,6},{14,10},{7,3},{... | collective-permute-start | bytes 786440 | tf_op jit(solution)/shard_map/ppermute | solution.py:18
  262.1 6.7 %copy-start.20 = (f32[8,1,128,128]{2,3,0,1:T(8,128)S(1)}, f32[8,1,128,128]{2,3,0,1:T(8,128)}, u32[]{:S(2)}) copy-start(f32[8,1,128,128]{2,3,0,1:T(8,128)} %copy.217) | copy-start | bytes 1572868
  278.9 5.6 %copy-start.5 = (f32[8,128,128]{1,2,0:T(8,128)S(1)}, f32[8,128,128]{1,2,0:T(8,128)}, u32[]{:S(2)}) copy-start(f32[8,128,128]{1,2,0:T(8,128)} %get-tuple-element.425) | copy-start | bytes 1572868
  (31 other events, 75.1 us)
Sparse Core Ops, SparseCore 0:
  17.9 8.2 all-gather.7
  31.0 93.0 all-gather.9
  144.8 112.2 all-gather.11
  281.4 17.6 all-reduce.6
where the time goes:
time: 315 us; the launch traced here: 309 us
  blocking collectives  152 us (48%)
  matrix products  56.4 us (18%)
  other arithmetic  30.4 us (10%)
  local copies, waits for them, and re-layouts  26 us (8%)
  between operations  15.3 us (5%)
  starting transfers between devices  14.5 us (5%)
  waiting for transfers between devices  13.9 us (4%)
    all_gather x2, blocking collectives, carried_in(): everything = jax.tree.map(lambda part: lax.all_gather(part, axis), value)  111 us
    all_gather x1, blocking collectives, local(): lax.all_gather(value_half, 'ctx', axis=0, tiled=True)  23.5 us
    unnamed x94, local copies, waits for them, and re-layouts  19.2 us
    all_gather x1, blocking collectives, local(): lax.all_gather(key_half, 'ctx', axis=0, tiled=True)  18.2 us
    ppermute x6, starting transfers between devices, from_behind(): lax.ppermute(value, axis, [(source, source + steps) for source in range(l...  13.7 us
    select_n x16, other arithmetic, hop(): return jax.tree.map(lambda a, b: jnp.where(reached, a, b), new, before)  12.8 us
    psum x1, waiting for transfers between devices, local(): key_grad, value_grad = lax.psum((key_local, value_local), 'sub')  12.4 us
  transfers between devices with their start and end apart: 13, of which 2 were waited for; matrix products, arithmetic and copies ran while one was open for 31% of the time, Pallas kernels for 0%

commit v1 on v0

v1 whole, which is shorter than its diff:
```python
import functools
import math

import jax
import jax.numpy as jnp
from jax import lax
from jax.experimental import pallas as pl
from jax.experimental.pallas import tpu as pltpu
from jax.sharding import PartitionSpec as P

NEG = -1e30
F32 = jnp.float32
BF16 = jnp.bfloat16

NT = (((1,), (1,)), ((), ()))
NN = (((1,), (0,)), ((), ()))


def shifted(value, axis, steps):
    count = lax.axis_size(axis)
    first, last = max(0, -steps), min(count, count - steps)
    return lax.ppermute(value, axis, [(i, i + steps) for i in range(first, last)])


def split2(x):
    hi = x.astype(BF16)
    return hi, (x - hi.astype(F32)).astype(BF16)


def split3(x):
    hi = x.astype(BF16)
    rest = x - hi.astype(F32)
    mid = rest.astype(BF16)
    return hi, mid, (rest - mid.astype(F32)).astype(BF16)


def dot(a, b, dims):
    return lax.dot_general(a, b, dims, preferred_element_type=F32)


def mm3(a, b, dims):
    return dot(a[0], b[0], dims) + (dot(a[0], b[1], dims) + dot(a[1], b[0], dims))


def mm6(a, b, dims):
    small = dot(a[0], b[2], dims) + dot(a[2], b[0], dims) + dot(a[1], b[1], dims)
    return dot(a[0], b[0], dims) + (dot(a[0], b[1], dims) + dot(a[1], b[0], dims) + small)


def colsum(x):
    return jnp.sum(x, axis=0, keepdims=True)


def softmax_pair(mapped):
    up = jnp.exp(mapped - jnp.max(mapped, axis=0, keepdims=True))
    low = jnp.exp(jnp.min(mapped, axis=0, keepdims=True) - mapped)
    return up * (1.0 / colsum(up)), low * (1.0 / colsum(low))


def softmax_pair_back(feat, grad, width):
    up, low = feat[:width], feat[width:]
    gup, glow = grad[:width], grad[width:]
    return up * (gup - colsum(up * gup)) - low * (glow - colsum(low * glow))


def pack_kernel(cfg, idx_ref, q_ref, k_ref, v_ref, q4_ref, kv_ref):
    sub = idx_ref[1]
    for g in range(cfg.groups):
        for h in range(cfg.per_group):
            rows = pl.ds(h * cfg.tokens, cfg.tokens)
            q4_ref[g, rows, :] = q_ref[:, g * cfg.per_group + h, :]
        for slot, ref in enumerate((k_ref, v_ref)):
            value = ref[:, cfg.starts[0] + g, :]
            for s in range(1, len(cfg.starts)):
                value = jnp.where(sub == s, ref[:, cfg.starts[s] + g, :], value)
            kv_ref[g, slot] = value


def main_kernel(cfg, idx_ref, q4_ref, own_ref, *refs):
    far_in = refs[: cfg.devices - 1]
    refs = refs[cfg.devices - 1 :]
    wq_ref, wk_ref, dq_ref, down_ref = refs[:4]
    far_out = refs[4 : 4 + cfg.devices - 1]
    (kv_s, dkv_s, fq_s, mx_s, mass_s, tnum_s, num_s, den_s, c_s, fk_s, dfq_s, win_s) = refs[
        4 + cfg.devices - 1 :
    ]
    here = idx_ref[0]
    group = pl.program_id(0)
    tokens, width, per_group = cfg.tokens, cfg.width, cfg.per_group
    rows = per_group * tokens
    scale = 1.0 / math.sqrt(width)

    for k in range(1, cfg.devices):
        kv_s[k] = far_in[k - 1][0]
    kv_s[0] = own_ref[0]

    query = q4_ref[0] * scale
    query_3 = split3(query)
    wk_t = split3(
        jnp.concatenate([wk_ref[h].T for h in range(per_group)], axis=0)
    )

    def head(x, h):
        return x[:, h * tokens : (h + 1) * tokens]

    raw_3 = split3(q4_ref[0])
    for h in range(per_group):
        wq_t = split3(wq_ref[h].T)
        piece = tuple(x[h * tokens : (h + 1) * tokens] for x in raw_3)
        up, low = softmax_pair(mm6(wq_t, piece, NT))
        fq_s[h, :width] = up
        fq_s[h, width:] = low

    key_row = lax.broadcasted_iota(jnp.int32, (tokens, rows), 0)
    query_col = lax.broadcasted_iota(jnp.int32, (tokens, rows), 1) % tokens
    seen = key_row <= query_col
    s_own = jnp.where(seen, mm6(split3(kv_s[0, 0]), query_3, NT), NEG)
    s_prev = jnp.where(here > 0, mm6(split3(kv_s[1, 0]), query_3, NT), NEG)
    top = jnp.maximum(
        jnp.max(s_own, axis=0, keepdims=True), jnp.max(s_prev, axis=0, keepdims=True)
    )
    a_own = jnp.exp(s_own - top)
    a_prev = jnp.exp(s_prev - top)
    mass = colsum(a_own) + colsum(a_prev)
    win_s[0] = a_own
    win_s[1] = a_prev
    wnum = mm3(split2(kv_s[0, 1].T), split2(a_own), NN) + mm3(
        split2(kv_s[1, 1].T), split2(a_prev), NN
    )
    mx_s[...] = top
    mass_s[...] = mass
    tnum_s[...] = wnum
    num_s[...] = wnum
    den_s[...] = mass

    def far_forward(k, carry):
        key, value = kv_s[k, 0], kv_s[k, 1]
        key_3 = split3(key)
        value_t = split2(value.T)
        s = mm6(key_3, query_3, NT)
        old = mx_s[...]
        new = jnp.maximum(old, jnp.max(s, axis=0, keepdims=True))
        p = jnp.exp(s - new)
        factor = jnp.exp(old - new)
        mx_s[...] = new
        mass_s[...] = mass_s[...] * factor + colsum(p)
        tnum_s[...] = tnum_s[...] * factor + mm3(value_t, split2(p), NN)
        mapped = mm6(wk_t, key_3, NT)
        for h in range(per_group):
            up, low = softmax_pair(mapped[h * width : (h + 1) * width])
            fk_t = jnp.concatenate([up, low], axis=0)
            fk_s[k, h] = fk_t
            c_s[k, :, h * tokens : (h + 1) * tokens] = mm3(
                split2(fk_t.T), split2(fq_s[h]), NN
            )
        c = c_s[k]
        num_s[...] += mm3(value_t, split2(c), NN)
        den_s[...] += colsum(c)
        return carry

    lax.fori_loop(2, here + 1, far_forward, 0)

    inv = 1.0 / den_s[...]
    out = num_s[...] * inv
    residual = out - tnum_s[...] * (1.0 / mass_s[...])
    grad = residual * inv
    grad_2 = split2(grad)
    grad_den = -colsum(residual * out) * inv
    query_2 = split2(query)

    dq = jnp.zeros((width, rows), F32)
    for slot in range(2):
        a = win_s[slot]
        soft = a * (mm3(split2(kv_s[slot, 1]), grad_2, NN) + grad_den)
        soft_2 = split2(soft)
        dkv_s[slot, 0] = mm3(soft_2, query_2, NN)
        dkv_s[slot, 1] = mm3(split2(a), grad_2, NT)
        dq = dq + mm3(split2(kv_s[slot, 0].T), soft_2, NN)
    dq = dq * scale

    dfq_s[...] = jnp.zeros_like(dfq_s)
    wk_2 = split2(jnp.concatenate([wk_ref[h] for h in range(per_group)], axis=1))

    def far_backward(k, carry):
        value = kv_s[k, 1]
        dc = mm3(split2(value), grad_2, NN) + grad_den
        dc_2 = split2(dc)
        dkv_s[k, 1] = mm3(split2(c_s[k]), grad_2, NT)
        pieces = []
        for h in range(per_group):
            fk_t = fk_s[k, h]
            dc_h = tuple(head(x, h) for x in dc_2)
            dfq_s[h] += mm3(split2(fk_t), dc_h, NN)
            dfk = mm3(split2(fq_s[h]), dc_h, NT)
            pieces.append(softmax_pair_back(fk_t, dfk, width))
        dkv_s[k, 0] = mm3(wk_2, split2(jnp.concatenate(pieces, axis=0)), NN).T
        return carry

    lax.fori_loop(2, here + 1, far_backward, 0)

    for h in range(per_group):
        back = softmax_pair_back(fq_s[h], dfq_s[h], width)
        dq_h = (head(dq, h) + mm3(split2(wq_ref[h]), split2(back), NN)).T
        for g in range(cfg.groups):

            @pl.when(group == g)
            def _():
                dq_ref[:, g * per_group + h, :] = dq_h

    down_ref[0] = dkv_s[0]
    for k in range(1, cfg.devices):

        @pl.when(here >= k)
        def _():
            far_out[k - 1][0] = dkv_s[k]

        @pl.when(here < k)
        def _():
            far_out[k - 1][0] = jnp.zeros_like(dkv_s[k])


def add_kernel(*refs):
    total = refs[0][...]
    for ref in refs[1:-1]:
        total = total + ref[...]
    refs[-1][...] = total


def place_kernel(cfg, idx_ref, mine_ref, other_ref, dk_ref, dv_ref):
    sub = idx_ref[1]
    for slot, ref in enumerate((dk_ref, dv_ref)):
        for g in range(cfg.groups_dev):
            if cfg.shared:
                ref[:, g, :] = mine_ref[g, slot] + other_ref[g, slot]
            else:
                owner = g // cfg.groups
                local_g = g % cfg.groups
                ref[:, g, :] = jnp.where(
                    sub == owner, mine_ref[local_g, slot], other_ref[local_g, slot]
                )


class Config:
    def __init__(self, queries, key_vectors):
        self.tokens, self.heads, self.width = queries.shape
        self.groups_dev = key_vectors.shape[1]
        self.devices = lax.axis_size("ctx")
        subs = lax.axis_size("sub")
        assert subs == 2
        size = self.heads * subs // self.groups_dev
        self.shared = self.heads < size
        self.groups = max(1, self.heads // size)
        self.per_group = self.heads // self.groups
        self.starts = [s * self.heads // size for s in range(subs)]
        if self.shared:
            assert self.groups_dev == 1


VMEM = pl.BlockSpec(memory_space=pltpu.VMEM)
SMEM = pl.BlockSpec(memory_space=pltpu.SMEM)


def local(queries, key_vectors, value_vectors, query_feature, key_feature):
    cfg = Config(queries, key_vectors)
    tokens, width, groups, per_group = cfg.tokens, cfg.width, cfg.groups, cfg.per_group
    n, rows = cfg.devices, cfg.per_group * cfg.tokens
    idx = jnp.stack([lax.axis_index("ctx"), lax.axis_index("sub")]).astype(jnp.int32)
    kv_shape = jax.ShapeDtypeStruct((groups, 2, tokens, width), F32)
    q4, own = pl.pallas_call(
        functools.partial(pack_kernel, cfg),
        name="pack",
        out_shape=(jax.ShapeDtypeStruct((groups, rows, width), F32), kv_shape),
        in_specs=[SMEM, VMEM, VMEM, VMEM],
        out_specs=(VMEM, VMEM),
    )(idx, queries, key_vectors, value_vectors)
    far = [shifted(own, "ctx", k) for k in range(1, n)]

    kv_spec = pl.BlockSpec((1, 2, tokens, width), lambda g: (g, 0, 0, 0))
    w_spec = pl.BlockSpec((per_group, width, width), lambda g: (g, 0, 0))
    scratch = [
        pltpu.VMEM((n, 2, tokens, width), F32),
        pltpu.VMEM((n, 2, tokens, width), F32),
        pltpu.VMEM((per_group, 2 * width, tokens), F32),
        pltpu.VMEM((1, rows), F32),
        pltpu.VMEM((1, rows), F32),
        pltpu.VMEM((width, rows), F32),
        pltpu.VMEM((width, rows), F32),
        pltpu.VMEM((1, rows), F32),
        pltpu.VMEM((n, tokens, rows), F32),
        pltpu.VMEM((n, per_group, 2 * width, tokens), F32),
        pltpu.VMEM((per_group, 2 * width, tokens), F32),
        pltpu.VMEM((2, tokens, rows), F32),
    ]
    results = pl.pallas_call(
        functools.partial(main_kernel, cfg),
        name="attend",
        grid=(groups,),
        out_shape=(jax.ShapeDtypeStruct(queries.shape, F32), kv_shape) + (kv_shape,) * (n - 1),
        in_specs=[SMEM, pl.BlockSpec((1, rows, width), lambda g: (g, 0, 0)), kv_spec]
        + [kv_spec] * (n - 1)
        + [w_spec, w_spec],
        out_specs=(pl.BlockSpec(queries.shape, lambda g: (0, 0, 0)), kv_spec)
        + (kv_spec,) * (n - 1),
        scratch_shapes=scratch,
        compiler_params=pltpu.CompilerParams(dimension_semantics=("arbitrary",)),
    )(idx, q4, own, *far, query_feature, key_feature)
    query_grad, mine = results[:2]
    back = [shifted(results[1 + k], "ctx", -k) for k in range(1, n)]
    mine = pl.pallas_call(
        add_kernel,
        name="add",
        out_shape=kv_shape,
        in_specs=[VMEM] * n,
        out_specs=VMEM,
    )(mine, *back)
    other = lax.ppermute(mine, "sub", [(0, 1), (1, 0)])
    key_grad, value_grad = pl.pallas_call(
        functools.partial(place_kernel, cfg),
        name="place",
        out_shape=(
            jax.ShapeDtypeStruct(key_vectors.shape, F32),
            jax.ShapeDtypeStruct(value_vectors.shape, F32),
        ),
        in_specs=[SMEM, VMEM, VMEM],
        out_specs=(VMEM, VMEM),
    )(idx, mine, other)
    return query_grad, key_grad, value_grad


def solution(mesh):
    placed = (
        P(("groups", "ctx"), ("head", "sub"), None),
        P(("groups", "ctx"), "head", None),
        P(("groups", "ctx"), "head", None),
        P(("head", "sub"), None, None),
        P(("head", "sub"), None, None),
    )
    return jax.shard_map(
        local,
        mesh=mesh,
        in_specs=placed,
        out_specs=placed[:3],
        check_vma=False,
    )
```

time: 315 us -> 87.6 us (0.28); the launches traced: 309 us -> 87.3 us
  blocking collectives: 152 us -> 0 us
  matrix products: 56.4 us -> 0 us
  waiting for transfers between devices: 13.9 us -> 51.9 us
  other arithmetic: 30.4 us -> 0.6 us
  local copies, waits for them, and re-layouts: 26 us -> 2.17 us
  Pallas kernels: 0 us -> 17.3 us
  between operations: 15.3 us -> 0.7 us
    all_gather x4 -> x0, blocking collectives: 152 us -> none  [the longest x2 111 us: carried_in(): everything = jax.tree.map(lambda part: lax.all_gather(part, axis), value)]
    dot_general x28 -> x0, matrix products: 56.4 us -> none  [the longest x1 4.55 us: one_block(): jnp.einsum('ltd,lnd->ltn', query_heads, keys_heads, precision=highest)]
    ppermute x9 -> x7, waiting for transfers between devices: 1.41 us -> 51.9 us  [the longest x6 50.1 us: shifted(): lax.ppermute(value, axis, [(i, i + steps) for i in range(first, last)])]
    pallas_call x0 -> x4, Pallas kernels: none -> 17.3 us  [the longest x1 10.8 us: local(): pl.pallas_call(functools.partial(main_kernel, cfg), name='attend', grid=(...]
    unnamed x94 -> x14, local copies, waits for them, and re-layouts: 19.2 us -> 2.17 us
    select_n x20 -> x0, other arithmetic: 13 us -> none  [the longest x16 12.8 us: hop(): return jax.tree.map(lambda a, b: jnp.where(reached, a, b), new, before)]
    psum x1 -> x0, waiting for transfers between devices: 12.4 us -> none  [local(): key_grad, value_grad = lax.psum((key_local, value_local), 'sub')]
    sub x8 -> x0, other arithmetic: 7.28 us -> none  [the longest x1 2.13 us: features_back(): upper = jax.nn.softmax(mapped, axis=-1)]
  transfers between devices with their start and end apart: 13 -> 7, of which waited for: 2 -> 6; matrix products, arithmetic and copies ran while one was open for 31% -> 0% of each run, Pallas kernels for 0% -> 0%
where the time goes in v1:
time: 87.6 us; the launch traced here: 87.3 us
  waiting for transfers between devices  51.9 us (59%)
  Pallas kernels  17.3 us (20%)
  starting transfers between devices  14.6 us (17%)
  local copies, waits for them, and re-layouts  2.17 us (2%)
    ppermute x6, waiting for transfers between devices, shifted(): lax.ppermute(value, axis, [(i, i + steps) for i in range(first, last)])  50.1 us
    ppermute x6, starting transfers between devices, shifted(): lax.ppermute(value, axis, [(i, i + steps) for i in range(first, last)])  14.6 us
    pallas_call x1, Pallas kernels, local(): pl.pallas_call(functools.partial(main_kernel, cfg), name='attend', grid=(...  10.8 us
    pallas_call x1, Pallas kernels, local(): pl.pallas_call(functools.partial(pack_kernel, cfg), name='pack', out_shap...  2.58 us
    unnamed x14, local copies, waits for them, and re-layouts  2.17 us
    pallas_call x1, Pallas kernels, local(): pl.pallas_call(functools.partial(place_kernel, cfg), name='place', out_sh...  2.05 us
    pallas_call x1, Pallas kernels, local(): pl.pallas_call(add_kernel, name='add', out_shape=kv_shape, in_specs=[VMEM...  1.93 us
  transfers between devices with their start and end apart: 7, of which 6 were waited for; matrix products, arithmetic and copies ran while one was open for 0% of the time, Pallas kernels for 0%

profile of v1, /device:TPU:0, one launch (start us, length us, event | category | flops | bytes accessed | tf_op | source)
XLA Modules:
  0.0 87.3 jit_solution(14877276083661952286)
XLA Ops:
  0.6 0.6 pad_add_fusion.idx_ref
  1.2 2.6 %pack.1 = (f32[2,512,128]{2,1,0:T(8,128)}, f32[2,2,128,128]{3,2,1,0:T(8,128)}) custom-call(s32[2]{0:T(128)} %pad_add_fusion.idx_ref, f32[128,8,128]{2,1,0:T(8,128)} %q_ref.1, f32[128,4,128]{2,1,0:T(4,128)} %k_ref.1, f32[128,4,128]{2,1,0:T(4,128)} %v_ref.1), custom_call_target="tpu_custom_call" | custom-call | tf_op jit(solution)/shard_map/pack/pallas_call | solution.py:269
  3.8 7.0 %collective-permute-start.2 = (f32[2,2,128,128]{3,2,1,0:T(8,128)}, f32[2,2,128,128]{3,2,1,0:T(8,128)S(1)}, u32[]{:S(2)}, u32[]{:S(2)}) collective-permute-start(f32[2,2,128,128]{3,2,1,0:T(8,128)} %get-tuple-element.13.own_ref), channel_id=1, source_target_pairs={{0,12},{1,13},{2,14},{3,15},{16,28},{17,29},{18,30},{19,31}} | collective-permute-start | bytes 786440 | tf_op jit(solution)/shard_map/ppermute | solution.py:22
  10.8 1.3 %collective-permute-start.1 = (f32[2,2,128,128]{3,2,1,0:T(8,128)}, f32[2,2,128,128]{3,2,1,0:T(8,128)S(1)}, u32[]{:S(2)}, u32[]{:S(2)}) collective-permute-start(f32[2,2,128,128]{3,2,1,0:T(8,128)} %get-tuple-element.13.own_ref), channel_id=1, source_target_pairs={{0,8},{4,12},{1,9},{5,13},{2,10},{6,14},{3,11},{7,15},{16,24},{20,... | collective-permute-start | bytes 786440 | tf_op jit(solution)/shard_map/ppermute | solution.py:22
  12.1 2.5 %collective-permute-start = (f32[2,2,128,128]{3,2,1,0:T(8,128)}, f32[2,2,128,128]{3,2,1,0:T(8,128)S(1)}, u32[]{:S(2)}, u32[]{:S(2)}) collective-permute-start(f32[2,2,128,128]{3,2,1,0:T(8,128)} %get-tuple-element.13.own_ref), channel_id=1, source_target_pairs={{0,4},{4,8},{8,12},{1,5},{5,9},{9,13},{2,6},{6,10},{10,14},{3,7},{... | collective-permute-start | bytes 786440 | tf_op jit(solution)/shard_map/ppermute | solution.py:22
  14.6 3.3 %collective-permute-done.2.refs_2_ = f32[2,2,128,128]{3,2,1,0:T(8,128)S(1)} collective-permute-done((f32[2,2,128,128]{3,2,1,0:T(8,128)}, f32[2,2,128,128]{3,2,1,0:T(8,128)S(1)}, u32[]{:S(2)}, u32[]{:S(2)}) %collective-permute-start.2) | collective-permute-done | bytes 262176 | tf_op jit(solution)/shard_map/ppermute | solution.py:22
  17.9 5.6 %collective-permute-done.1.refs_1_ = f32[2,2,128,128]{3,2,1,0:T(8,128)S(1)} collective-permute-done((f32[2,2,128,128]{3,2,1,0:T(8,128)}, f32[2,2,128,128]{3,2,1,0:T(8,128)S(1)}, u32[]{:S(2)}, u32[]{:S(2)}) %collective-permute-start.1) | collective-permute-done | bytes 262176 | tf_op jit(solution)/shard_map/ppermute | solution.py:22
  23.5 4.5 %collective-permute-done.refs_0_ = f32[2,2,128,128]{3,2,1,0:T(8,128)S(1)} collective-permute-done((f32[2,2,128,128]{3,2,1,0:T(8,128)}, f32[2,2,128,128]{3,2,1,0:T(8,128)S(1)}, u32[]{:S(2)}, u32[]{:S(2)}) %collective-permute-start) | collective-permute-done | bytes 262176 | tf_op jit(solution)/shard_map/ppermute | solution.py:22
  28.0 0.0 copy-done.5
  28.0 0.7 copy-done.6
  28.7 10.8 %attend.1 = (f32[128,8,128]{2,1,0:T(8,128)}, f32[2,2,128,128]{3,2,1,0:T(8,128)}, f32[2,2,128,128]{3,2,1,0:T(8,128)}, f32[2,2,128,128]{3,2,1,0:T(8,128)}, f32[2,2,128,128]{3,2,1,0:T(8,128)}) custom-call(s32[2]{0:T(128)} %pad_add_fusion.idx_ref, f32[2,512,128]{2,1,0:T(8,128)} %get-tuple-element.12.q4_ref, f32[2,2,128,128]{3,2,1,0:T(8,128)} %get-tuple-element.13.own_ref, ...), custom_call_target="tpu_custom_call" | custom-call | tf_op jit(solution)/shard_map/attend/pallas_call | solution.py:294
  39.4 1.3 %collective-permute-start.3 = (f32[2,2,128,128]{3,2,1,0:T(8,128)}, f32[2,2,128,128]{3,2,1,0:T(8,128)S(1)}, u32[]{:S(2)}, u32[]{:S(2)}) collective-permute-start(f32[2,2,128,128]{3,2,1,0:T(8,128)} %get-tuple-element.16), channel_id=1, source_target_pairs={{4,0},{8,4},{12,8},{5,1},{9,5},{13,9},{6,2},{10,6},{14,10},{7,3},{... | collective-permute-start | bytes 786440 | tf_op jit(solution)/shard_map/ppermute | solution.py:22
  40.7 1.3 %collective-permute-start.4 = (f32[2,2,128,128]{3,2,1,0:T(8,128)}, f32[2,2,128,128]{3,2,1,0:T(8,128)S(1)}, u32[]{:S(2)}, u32[]{:S(2)}) collective-permute-start(f32[2,2,128,128]{3,2,1,0:T(8,128)} %get-tuple-element.17), channel_id=1, source_target_pairs={{8,0},{12,4},{9,1},{13,5},{10,2},{14,6},{11,3},{15,7},{24,16},{28,... | collective-permute-start | bytes 786440 | tf_op jit(solution)/shard_map/ppermute | solution.py:22
  42.0 1.3 %collective-permute-start.5 = (f32[2,2,128,128]{3,2,1,0:T(8,128)}, f32[2,2,128,128]{3,2,1,0:T(8,128)S(1)}, u32[]{:S(2)}, u32[]{:S(2)}) collective-permute-start(f32[2,2,128,128]{3,2,1,0:T(8,128)} %get-tuple-element.18), channel_id=1, source_target_pairs={{12,0},{13,1},{14,2},{15,3},{28,16},{29,17},{30,18},{31,19}} | collective-permute-start | bytes 786440 | tf_op jit(solution)/shard_map/ppermute | solution.py:22
  43.3 11.7 %collective-permute-done.3.refs_1_ = f32[2,2,128,128]{3,2,1,0:T(8,128)S(1)} collective-permute-done((f32[2,2,128,128]{3,2,1,0:T(8,128)}, f32[2,2,128,128]{3,2,1,0:T(8,128)S(1)}, u32[]{:S(2)}, u32[]{:S(2)}) %collective-permute-start.3) | collective-permute-done | bytes 262176 | tf_op jit(solution)/shard_map/ppermute | solution.py:22
  55.1 25.0 %collective-permute-done.4.refs_2_ = f32[2,2,128,128]{3,2,1,0:T(8,128)S(1)} collective-permute-done((f32[2,2,128,128]{3,2,1,0:T(8,128)}, f32[2,2,128,128]{3,2,1,0:T(8,128)S(1)}, u32[]{:S(2)}, u32[]{:S(2)}) %collective-permute-start.4) | collective-permute-done | bytes 262176 | tf_op jit(solution)/shard_map/ppermute | solution.py:22
  80.1 0.0 collective-permute-done.5.refs_3_
  80.1 0.7 copy-done.1
  80.8 0.1 copy-done.2
  80.8 1.9 %add.3.mine_ref = f32[2,2,128,128]{3,2,1,0:T(8,128)} custom-call(f32[2,2,128,128]{3,2,1,0:T(8,128)} %get-tuple-element.15.refs_0_, f32[2,2,128,128]{3,2,1,0:T(8,128)} %copy-done, f32[2,2,128,128]{3,2,1,0:T(8,128)} %copy-done.1, f32[2,2,128,128]{3,2,1,0:T(8,128)} %copy-done.2), custom_call_target="tpu_custom_call" | custom-call | tf_op jit(solution)/shard_map/add/pallas_call | solution.py:309
  82.8 0.0 collective-permute-start.6
  82.8 1.7 %collective-permute-done.6.other_ref = f32[2,2,128,128]{3,2,1,0:T(8,128)S(1)} collective-permute-done((f32[2,2,128,128]{3,2,1,0:T(8,128)}, f32[2,2,128,128]{3,2,1,0:T(8,128)S(1)}, u32[]{:S(2)}, u32[]{:S(2)}) %collective-permute-start.6) | collective-permute-done | bytes 262176 | tf_op jit(solution)/shard_map/ppermute | solution.py:316
  84.5 0.7 copy-done.3
  85.2 2.0 %place.1 = (f32[128,4,128]{2,1,0:T(4,128)}, f32[128,4,128]{2,1,0:T(4,128)}) custom-call(s32[2]{0:T(128)} %pad_add_fusion.idx_ref, f32[2,2,128,128]{3,2,1,0:T(8,128)} %add.3.mine_ref, f32[2,2,128,128]{3,2,1,0:T(8,128)} %copy-done.3), custom_call_target="tpu_custom_call" | custom-call | tf_op jit(solution)/shard_map/place/pallas_call | solution.py:317
  (9 shorter events, 0.0 us)
Async XLA Ops:
  3.8 14.1 %collective-permute-start.2 = (f32[2,2,128,128]{3,2,1,0:T(8,128)}, f32[2,2,128,128]{3,2,1,0:T(8,128)S(1)}, u32[]{:S(2)}, u32[]{:S(2)}) collective-permute-start(f32[2,2,128,128]{3,2,1,0:T(8,128)} %get-tuple-element.13.own_ref), channel_id=1, source_target_pairs={{0,12},{1,13},{2,14},{3,15},{16,28},{17,29},{18,30},{19,31}} | collective-permute-start | bytes 786440 | tf_op jit(solution)/shard_map/ppermute | solution.py:22
  10.8 12.7 %collective-permute-start.1 = (f32[2,2,128,128]{3,2,1,0:T(8,128)}, f32[2,2,128,128]{3,2,1,0:T(8,128)S(1)}, u32[]{:S(2)}, u32[]{:S(2)}) collective-permute-start(f32[2,2,128,128]{3,2,1,0:T(8,128)} %get-tuple-element.13.own_ref), channel_id=1, source_target_pairs={{0,8},{4,12},{1,9},{5,13},{2,10},{6,14},{3,11},{7,15},{16,24},{20,... | collective-permute-start | bytes 786440 | tf_op jit(solution)/shard_map/ppermute | solution.py:22
  12.1 15.9 %collective-permute-start = (f32[2,2,128,128]{3,2,1,0:T(8,128)}, f32[2,2,128,128]{3,2,1,0:T(8,128)S(1)}, u32[]{:S(2)}, u32[]{:S(2)}) collective-permute-start(f32[2,2,128,128]{3,2,1,0:T(8,128)} %get-tuple-element.13.own_ref), channel_id=1, source_target_pairs={{0,4},{4,8},{8,12},{1,5},{5,9},{9,13},{2,6},{6,10},{10,14},{3,7},{... | collective-permute-start | bytes 786440 | tf_op jit(solution)/shard_map/ppermute | solution.py:22
  17.9 10.1 %copy-start.4 = (f32[2,2,128,128]{3,2,1,0:T(8,128)}, f32[2,2,128,128]{3,2,1,0:T(8,128)S(1)}, u32[]{:S(2)}) copy-start(f32[2,2,128,128]{3,2,1,0:T(8,128)S(1)} %collective-permute-done.2.refs_2_) | copy-start | bytes 786436
  23.5 4.5 %copy-start.5 = (f32[2,2,128,128]{3,2,1,0:T(8,128)}, f32[2,2,128,128]{3,2,1,0:T(8,128)S(1)}, u32[]{:S(2)}) copy-start(f32[2,2,128,128]{3,2,1,0:T(8,128)S(1)} %collective-permute-done.1.refs_1_) | copy-start | bytes 786436
  28.0 0.7 copy-start.6
  39.4 15.6 %collective-permute-start.3 = (f32[2,2,128,128]{3,2,1,0:T(8,128)}, f32[2,2,128,128]{3,2,1,0:T(8,128)S(1)}, u32[]{:S(2)}, u32[]{:S(2)}) collective-permute-start(f32[2,2,128,128]{3,2,1,0:T(8,128)} %get-tuple-element.16), channel_id=1, source_target_pairs={{4,0},{8,4},{12,8},{5,1},{9,5},{13,9},{6,2},{10,6},{14,10},{7,3},{... | collective-permute-start | bytes 786440 | tf_op jit(solution)/shard_map/ppermute | solution.py:22
  40.7 39.3 %collective-permute-start.4 = (f32[2,2,128,128]{3,2,1,0:T(8,128)}, f32[2,2,128,128]{3,2,1,0:T(8,128)S(1)}, u32[]{:S(2)}, u32[]{:S(2)}) collective-permute-start(f32[2,2,128,128]{3,2,1,0:T(8,128)} %get-tuple-element.17), channel_id=1, source_target_pairs={{8,0},{12,4},{9,1},{13,5},{10,2},{14,6},{11,3},{15,7},{24,16},{28,... | collective-permute-start | bytes 786440 | tf_op jit(solution)/shard_map/ppermute | solution.py:22
  42.0 38.1 %collective-permute-start.5 = (f32[2,2,128,128]{3,2,1,0:T(8,128)}, f32[2,2,128,128]{3,2,1,0:T(8,128)S(1)}, u32[]{:S(2)}, u32[]{:S(2)}) collective-permute-start(f32[2,2,128,128]{3,2,1,0:T(8,128)} %get-tuple-element.18), channel_id=1, source_target_pairs={{12,0},{13,1},{14,2},{15,3},{28,16},{29,17},{30,18},{31,19}} | collective-permute-start | bytes 786440 | tf_op jit(solution)/shard_map/ppermute | solution.py:22
  55.1 25.0 %copy-start = (f32[2,2,128,128]{3,2,1,0:T(8,128)}, f32[2,2,128,128]{3,2,1,0:T(8,128)S(1)}, u32[]{:S(2)}) copy-start(f32[2,2,128,128]{3,2,1,0:T(8,128)S(1)} %collective-permute-done.3.refs_1_) | copy-start | bytes 786436
  80.1 0.7 copy-start.1
  80.1 0.8 copy-start.2
  82.8 1.7 %collective-permute-start.6 = (f32[2,2,128,128]{3,2,1,0:T(8,128)}, f32[2,2,128,128]{3,2,1,0:T(8,128)S(1)}, u32[]{:S(2)}, u32[]{:S(2)}) collective-permute-start(f32[2,2,128,128]{3,2,1,0:T(8,128)} %add.3.mine_ref), channel_id=1, source_target_pairs={{0,1},{1,0},{2,3},{3,2},{4,5},{5,4},{6,7},{7,6},{8,9},{9,8},{10,11... | collective-permute-start | bytes 786440 | tf_op jit(solution)/shard_map/ppermute | solution.py:316
  84.5 0.7 copy-start.3
